TPU v7x, 32 devices: a whole 2x2x4 slice. The times are simulated.
32 devices in a mesh: row: 8 (over y, x, core), col: 4 (over z).
Axes of the slice: x: 2, y: 2, z: 4, core: 2. Of those that a mesh axis runs over, the one named last changes fastest.
Arguments:
- student_in: bfloat16 [768, 8192], P('col', 'row'), may hold values from -6 to 6
- norm_gain: bfloat16 [8192], P('row'), may hold values from 0.099609375 to 1.8984375
- w_gate: bfloat16 [8192, 28672], P('row', 'col'), may hold values from -0.0625 to 0.0625
- w_up: bfloat16 [8192, 28672], P('row', 'col'), may hold values from -0.0625 to 0.0625
- w_down: bfloat16 [28672, 8192], P('col', 'row'), may hold values from -0.03125 to 0.03125
- teacher: bfloat16 [2, 768, 8192], P(None, 'col', 'row'), may hold values from -6 to 6
- layer_map: int32 [2], replicated, may hold values from 0 to 1, each once
Outputs:
- student_out: bfloat16 [768, 8192], P('col', 'row')
- match_loss: float32 [], replicated
Inputs may be any that keep to these rules, and one draw needn't show every extreme that they name: `layer_map`: a permutation of 0 to 1.
All inputs are finite; a program needn't handle non-finite values.
Results may differ from a plain program's by a relative error of at most 0.014.
Values may be sent and summed in bfloat16 or wider, within the bound.
A program may use at most 192 MiB of HBM per device.

v0:
```python
import jax
import jax.numpy as jnp
from jax import lax
from jax.sharding import PartitionSpec as P

D = 8192


def swiglu(both, width):
    return (jax.nn.silu(both[:, :width]) * both[:, width:]).astype(jnp.bfloat16)


def body(student_in, norm_gain, w_gate, w_up, w_down, teacher, layer_map):
    xf = student_in.astype(jnp.float32)
    squares = lax.psum(jnp.sum(xf * xf, axis=1), "row")
    mean_sq = squares / D
    normed = (
        xf * lax.rsqrt(mean_sq[:, None] + 1e-05) * norm_gain.astype(jnp.float32)[None, :]
    ).astype(jnp.bfloat16)
    all_rows = lax.all_gather(normed, "col", axis=0, tiled=True)
    width = w_gate.shape[1]
    piece = all_rows
    first = jnp.dot(piece, w_gate, preferred_element_type=jnp.float32)
    second = jnp.dot(piece, w_up, preferred_element_type=jnp.float32)
    mine = lax.psum_scatter(
        jnp.concatenate([first, second], axis=1).astype(jnp.bfloat16),
        "row",
        scatter_dimension=0,
        tiled=True,
    ).astype(jnp.float32)
    hidden_all = lax.all_gather(swiglu(mine, width), "row", axis=0, tiled=True)
    piece = hidden_all
    branch = lax.psum_scatter(
        jnp.dot(piece, w_down, preferred_element_type=jnp.float32).astype(jnp.bfloat16),
        "col",
        scatter_dimension=0,
        tiled=True,
    ).astype(jnp.float32)
    student_out = (xf + branch).astype(jnp.bfloat16)
    target = lax.dynamic_index_in_dim(teacher, layer_map[0], 0, keepdims=False).astype(jnp.float32)
    diff = student_out.astype(jnp.float32) - target
    total = lax.psum(jnp.sum(diff * diff), ("row", "col"))
    count_all = student_in.shape[0] * lax.axis_size("col") * D
    return (student_out, total / count_all)


def solution(mesh):
    placed = (
        P("col", "row"),
        P("row"),
        P("row", "col"),
        P("row", "col"),
        P("col", "row"),
        P(None, "col", "row"),
        P(),
    )
    return jax.shard_map(
        body, mesh=mesh, in_specs=placed, out_specs=(P("col", "row"), P()), check_vma=False
    )
```

profile of v0, /device:TPU:0, one launch (start us, length us, event | category | flops | bytes accessed | tf_op | source)
XLA Modules:
  0.0 428.6 jit_solution(13553694904345614874)
XLA Ops:
  7.2 0.0 all-gather.3.cloned.1.call-start
  7.2 1.2 fusion.1
  8.4 15.1 %psum.14 = f32[192]{0:T(256)S(1)} all-reduce(f32[192]{0:T(256)S(1)} %fusion.1), channel_id=1, replica_groups=mesh['row'=8,'col'=4] {'row'}, use_global_device_ids=true, to_apply=%region_1.0 | all-reduce | flops 192 | bytes 1536 | tf_op jit(solution)/shard_map/psum | solution.py:15
  23.5 0.7 convert_element_type.35
  24.2 1.9 fusion.3
  26.1 0.0 all-gather.3.cloned.1.call-update
  26.1 0.0 reduce-scatter.3.cloned.1.call-start
  26.2 36.5 %all-gather.3.cloned.1.call-done = bf16[768,1024]{1,0:T(8,128)(2,1)} async-done(((bf16[192,1024]{1,0:T(8,128)(2,1)}), bf16[768,1024]{1,0:T(8,128)(2,1)}) %all-gather.3.cloned.1.call-update) | async-done | bytes 1572880 | tf_op jit(solution)/shard_map/all_gather | solution.py:20
  62.7 0.0 copy-start.3
  62.7 17.3 %convolution_convert_fusion = bf16[768,7168]{1,0:T(8,128)(2,1)S(1)} fusion(bf16[768,1024]{1,0:T(8,128)(2,1)} %all-gather.3.cloned.1.call-done, bf16[1024,7168]{1,0:T(8,128)(2,1)} %param.10), kind=kOutput, calls=%fused_computation.1 | convolution fusion | flops 11279794176 | bytes 27262976 | tf_op jit(solution)/shard_map/dot_general | solution.py:24
  79.9 0.0 copy-done.3
  80.0 19.0 %convolution_convert_fusion.1 = bf16[768,7168]{1,0:T(8,128)(2,1)} fusion(bf16[768,1024]{1,0:T(8,128)(2,1)S(1)} %copy-done.3, bf16[1024,7168]{1,0:T(8,128)(2,1)} %param.9), kind=kOutput, calls=%fused_computation.2 | convolution fusion | flops 11279794176 | bytes 27262976 | tf_op jit(solution)/shard_map/dot_general | solution.py:23
  98.9 16.5 %pad_maximum_fusion = bf16[768,14336]{1,0:T(8,128)(2,1)} fusion(bf16[768,7168]{1,0:T(8,128)(2,1)S(1)} %convolution_convert_fusion, bf16[768,7168]{1,0:T(8,128)(2,1)} %convolution_convert_fusion.1), kind=kLoop, calls=%fused_computation | loop fusion | flops 44040192 | bytes 44040192 | tf_op jit(solution)/shard_map/concatenate | solution.py:26
  115.4 0.0 reduce-scatter.3.cloned.1.call-update
  115.4 0.0 all-gather.5.cloned.1.call-start
  115.5 140.1 %reduce-scatter.3.cloned.1.call-done = bf16[96,14336]{1,0:T(8,128)(2,1)} async-done(((bf16[768,14336]{1,0:T(8,128)(2,1)}), bf16[96,14336]{1,0:T(8,128)(2,1)}) %reduce-scatter.3.cloned.1.call-update) | async-done | bytes 2752528 | tf_op jit(solution)/shard_map/reduce_scatter | solution.py:25
  255.5 2.3 convert_element_type.37
  257.8 1.8 fusion
  259.6 0.0 all-gather.5.cloned.1.call-update
  259.6 0.0 copy-start.2
  259.6 0.0 copy-start
  259.6 0.0 copy-start.1
  259.6 0.2 reduce-scatter.5.cloned.1.call-start
  259.9 65.2 %all-gather.5.cloned.1.call-done = bf16[768,7168]{1,0:T(8,128)(2,1)} async-done(((bf16[96,7168]{1,0:T(8,128)(2,1)}), bf16[768,7168]{1,0:T(8,128)(2,1)}) %all-gather.5.cloned.1.call-update) | async-done | bytes 11010064 | tf_op jit(solution)/shard_map/all_gather | solution.py:31
  325.1 17.8 %convolution_convert_fusion.2 = bf16[768,1024]{1,0:T(8,128)(2,1)} fusion(bf16[768,7168]{1,0:T(8,128)(2,1)} %all-gather.5.cloned.1.call-done, bf16[7168,1024]{1,0:T(8,128)(2,1)} %param.11), kind=kOutput, calls=%fused_computation.5 | convolution fusion | flops 11275075584 | bytes 27262976 | tf_op jit(solution)/shard_map/dot_general | solution.py:34
  342.9 0.0 reduce-scatter.5.cloned.1.call-update
  342.9 0.0 copy-done.2
  343.0 35.5 %reduce-scatter.5.cloned.1.call-done = bf16[192,1024]{1,0:T(8,128)(2,1)} async-done(((bf16[768,1024]{1,0:T(8,128)(2,1)}), bf16[192,1024]{1,0:T(8,128)(2,1)}) %reduce-scatter.5.cloned.1.call-update) | async-done | bytes 393232 | tf_op jit(solution)/shard_map/reduce_scatter | solution.py:33
  378.5 0.0 copy-done
  378.5 0.0 copy-done.1
  378.5 2.5 fusion.6
  381.0 39.2 %psum.15 = f32[]{:T(128)} all-reduce(f32[]{:T(128)} %get-tuple-element.2), channel_id=1, replica_groups=mesh['row'=8,'col'=4] {'row','col'}, use_global_device_ids=true, to_apply=%region_5.6 | all-reduce | flops 1 | bytes 8 | tf_op jit(solution)/shard_map/psum | solution.py:42
  (1 shorter events, 0.0 us)
Async XLA Ops:
  7.2 55.5 %all-gather.3.cloned.1.call-start = ((), (), s32[]{:S(2)}) async-start(), calls=%async_computation.2 | async-start | bytes 1966080 | tf_op jit(solution)/shard_map/all_gather | solution.py:20
  26.1 229.4 %reduce-scatter.3.cloned.1.call-start = ((), (), s32[]{:S(2)}) async-start(), calls=%async_computation.3 | async-start | bytes 24772608 | tf_op jit(solution)/shard_map/reduce_scatter | solution.py:25
  62.7 17.3 %copy-start.3 = (bf16[768,1024]{1,0:T(8,128)(2,1)S(1)}, bf16[768,1024]{1,0:T(8,128)(2,1)}, u32[]{:S(2)}) copy-start(bf16[768,1024]{1,0:T(8,128)(2,1)} %all-gather.3.cloned.1.call-done) | copy-start | bytes 4718596
  115.4 209.7 %all-gather.5.cloned.1.call-start = ((), (), s32[]{:S(2)}) async-start(), calls=%async_computation.4 | async-start | bytes 12386304 | tf_op jit(solution)/shard_map/all_gather | solution.py:31
  259.6 83.3 %copy-start.2 = (s32[2]{0:T(128)S(1)}, s32[2]{0:T(128)}, u32[]{:S(2)}) copy-start(s32[2]{0:T(128)} %param.13) | copy-start | bytes 28
  259.6 118.9 %copy-start = (bf16[192,1024]{1,0:T(8,128)(2,1)S(1)}, bf16[192,1024]{1,0:T(8,128)(2,1)}, u32[]{:S(2)}) copy-start(bf16[192,1024]{1,0:T(8,128)(2,1)} %param.7) | copy-start | bytes 1179652
  259.6 118.9 %copy-start.1 = (bf16[2,192,1024]{2,1,0:T(8,128)(2,1)S(1)}, bf16[2,192,1024]{2,1,0:T(8,128)(2,1)}, u32[]{:S(2)}) copy-start(bf16[2,192,1024]{2,1,0:T(8,128)(2,1)} %param.12) | copy-start | bytes 2359300
  259.6 118.8 %reduce-scatter.5.cloned.1.call-start = ((), (), s32[]{:S(2)}) async-start(), calls=%async_computation.5 | async-start | bytes 1966080 | tf_op jit(solution)/shard_map/reduce_scatter | solution.py:33
Sparse Core Ops, SparseCore 0:
  26.3 36.3 all-gather.2
  115.5 139.9 reduce-scatter.2
  259.7 65.3 all-gather.4
  343.0 35.4 reduce-scatter.4
where the time goes:
time: 429 us
  waiting for transfers between devices  277 us (65%)
  blocking collectives  54.4 us (13%)
  matrix products  54 us (13%)
  other arithmetic  26.8 us (6%)
  between operations  15.7 us (4%)
    reduce_scatter x1, waiting for transfers between devices, body(): lax.psum_scatter(jnp.concatenate([first, second], axis=1).astype(jnp.bflo...  140 us
    all_gather x1, waiting for transfers between devices, body(): hidden_all = lax.all_gather(swiglu(mine, width), 'row', axis=0, tiled=True)  65.2 us
    psum x1, blocking collectives, body(): total = lax.psum(jnp.sum(diff * diff), ('row', 'col'))  39.2 us
    all_gather x1, waiting for transfers between devices, body(): all_rows = lax.all_gather(normed, 'col', axis=0, tiled=True)  36.5 us
    reduce_scatter x1, waiting for transfers between devices, body(): lax.psum_scatter(jnp.dot(piece, w_down, preferred_element_type=jnp.float3...  35.5 us
    dot_general x1, matrix products, body(): first = jnp.dot(piece, w_gate, preferred_element_type=jnp.float32)  19 us
    dot_general x1, matrix products, body(): jnp.dot(piece, w_down, preferred_element_type=jnp.float32)  17.8 us
    dot_general x1, matrix products, body(): second = jnp.dot(piece, w_up, preferred_element_type=jnp.float32)  17.3 us
  transfers between devices with their start and end apart: 4, of which 4 were waited for; matrix products, arithmetic and copies ran while one was open for 0% of the time, Pallas kernels for 0%

commit v1 on v0

v1 whole, which is shorter than its diff:
```python
import functools

import jax
import jax.numpy as jnp
from jax import lax
from jax.experimental import pallas as pl
from jax.experimental.pallas import tpu as pltpu
from jax.sharding import PartitionSpec as P

BF = jnp.bfloat16
F32 = jnp.float32


def kernel(nr, nz, w, total, x_ref, gain_ref, wg_ref, wu_ref, wd_ref, teacher_ref, map_ref,
           out_ref, loss_ref,
           x_all, xg, ss, ssr, scale, wgu, wdn, p_own, p_send, s_in, half_send, half_in,
           full_send, full_in, h_all, acc, cs_r, cs_l, cr_r, cr_l, lsum, l_row, l_col,
           x_sems, w_sem, wd_sem, ss_sems, sib_sems, rs_send, rs_recv, ag_send, ag_recv,
           hs_send, hs_recv, c_sems, l_sems):
    n = nr // 2
    hn = n // 2
    chunks = s_in.shape[0]
    tr, feat = x_ref.shape
    g = tr * nz // nr
    hg = g // 2
    r = lax.axis_index("row")
    z = lax.axis_index("col")
    core = lax.rem(r, 2)
    chip = lax.div(r, 2)
    a, b = lax.div(chip, 2), lax.rem(chip, 2)
    pos = a + b * (n - 1 - 2 * a)

    def chip_at(off):
        q = lax.rem(pos + (off % n), n)
        far = lax.div(q, hn)
        return far * (2 * (n - 1 - q) + 1) + (1 - far) * 2 * q

    me = chip_at(0)
    sibling = {"row": chip * 2 + 1 - core}
    ring = ({"row": chip_at(1) * 2 + core}, {"row": chip_at(-1) * 2 + core})
    sign = (1, -1)
    rows_of = (pl.ds(0, hg), pl.ds(hg, hg))

    def remote(src, dst, send, recv, dev):
        return pltpu.make_async_remote_copy(
            src_ref=src, dst_ref=dst, send_sem=send, recv_sem=recv,
            device_id=dev, device_id_type=pl.DeviceIdType.MESH)

    barrier = pltpu.get_barrier_semaphore()
    for d in range(1, nr):
        pl.semaphore_signal(barrier, inc=1, device_id={"row": lax.rem(r + d, nr)},
                            device_id_type=pl.DeviceIdType.MESH)
    for d in range(1, nz):
        pl.semaphore_signal(barrier, inc=1, device_id={"col": lax.rem(z + d, nz)},
                            device_id_type=pl.DeviceIdType.MESH)
    pl.semaphore_wait(barrier, nr - 1 + nz - 1)

    def up_load(j):
        slot = lax.rem(j, 2)
        cols = pl.ds(pl.multiple_of(j * w, w), w)
        return (pltpu.make_async_copy(wg_ref.at[:, cols], wgu.at[slot, :, pl.ds(0, w)], w_sem.at[slot, 0]),
                pltpu.make_async_copy(wu_ref.at[:, cols], wgu.at[slot, :, pl.ds(w, w)], w_sem.at[slot, 1]))

    def down_load(j):
        slot = lax.rem(j, 2)
        return pltpu.make_async_copy(wd_ref.at[pl.ds(pl.multiple_of(j * w, w), w)], wdn.at[slot], wd_sem.at[slot])

    for c in up_load(jnp.int32(0)):
        c.start()
    down_load(jnp.int32(0)).start()

    gain = gain_ref[...].astype(F32)

    def absorb(src, blk):
        xf = src[...].astype(F32)
        rows = pl.ds(pl.multiple_of(blk * tr, tr), tr)
        xg[rows, :] = (xf * gain).astype(BF)
        sq = xf * xf
        part = sq[:, 0:128]
        for c in range(1, feat // 128):
            part = part + sq[:, c * 128:(c + 1) * 128]
        ss[rows, :] = part

    def x_copy(s, d):
        blk = z - s * sign[d]
        src = x_ref if s == 0 else x_all.at[blk]
        return remote(src, x_all.at[blk], x_sems.at[0, d, s], x_sems.at[1, d, s], {"col": z + sign[d]})

    def x_sends(s, d):
        return (z < nz - 1) & (z - s >= 0) if d == 0 else (z > 0) & (z + s <= nz - 1)

    def x_gets(s, d):
        return z - 1 - s >= 0 if d == 0 else z + 1 + s <= nz - 1

    def x_wait(s, d):
        blk = z - (s + 1) * sign[d]
        remote(x_all.at[blk], x_all.at[blk], x_sems.at[0, d, s], x_sems.at[1, d, s],
               {"col": z - sign[d]}).wait_recv()

    for s in range(nz - 1):
        for d in range(2):
            @pl.when(x_sends(s, d))
            def _():
                x_copy(s, d).start()
        if s == 0:
            absorb(x_ref, z)
        else:
            for d in range(2):
                @pl.when(x_gets(s - 1, d))
                def _():
                    absorb(x_all.at[z - s * sign[d]], z - s * sign[d])
        for d in range(2):
            @pl.when(x_gets(s, d))
            def _():
                x_wait(s, d)
    for d in range(2):
        @pl.when(x_gets(nz - 2, d))
        def _():
            absorb(x_all.at[z - (nz - 1) * sign[d]], z - (nz - 1) * sign[d])

    def ss_copy(d):
        peer = lax.rem(r + d, nr)
        return remote(ss.at[pl.ds(pl.multiple_of(peer * g, g), g)], ssr.at[d - 1],
                      ss_sems.at[0, d - 1], ss_sems.at[1, d - 1], {"row": peer})

    for d in range(1, nr):
        ss_copy(d).start()

    def sib(j):
        slot = lax.rem(j, 2)
        return remote(p_send.at[slot], s_in.at[j], sib_sems.at[slot], sib_sems.at[2 + j], sibling)

    def rs(s, d, j):
        slot = lax.rem(j, 2)
        if s == 0:
            src, dst = half_send.at[slot, d], half_in.at[j, d]
        else:
            src, dst = full_send.at[slot, s - 1, d], full_in.at[j, s - 1, d]
        return remote(src, dst, rs_send.at[s, d, slot], rs_recv.at[s, d, j], ring[d])

    def ag(s, d, j, got=False):
        blk = chip_at(-sign[d] * (s + 1 if got else s))
        ref = h_all.at[j, blk, core]
        if s == hn - 1:
            ref = h_all.at[j, blk, core, rows_of[d]]
        return remote(ref, ref, ag_send.at[s, d, lax.rem(j, 2)], ag_recv.at[s, d, j], ring[d])

    def hs(off, j, got=False):
        ref = h_all.at[j, chip_at(off), 1 - core if got else core]
        return remote(ref, ref, hs_send.at[off % n, lax.rem(j, 2)], hs_recv.at[off % n, j], sibling)

    def free(make, j):
        @pl.when(j >= 2)
        def _():
            make(j - 2).wait_send()

    def mine(j, off, rows=slice(None)):
        q = chip_at(off)
        return (p_own[lax.rem(j, hn + 2), q, rows, :].astype(F32) + s_in[j, q, rows, :].astype(F32))

    def first(j):
        slot = lax.rem(j, 2)

        @pl.when(j + 1 < chunks)
        def _():
            for c in up_load(j + 1):
                c.start()
        for c in up_load(j):
            c.wait()
        free(sib, j)
        tile = 256

        @pl.loop(0, 2 * w // tile)
        def _(t):
            cols = pl.ds(pl.multiple_of(t * tile, tile), tile)
            res = jnp.dot(xg[...], wgu[slot, :, cols], preferred_element_type=F32).astype(BF)
            res = res.reshape(n, 2, g, tile)

            @pl.when(core == 0)
            def _():
                p_own[lax.rem(j, hn + 2), :, :, cols] = res[:, 0]
                p_send[slot, :, :, cols] = res[:, 1]

            @pl.when(core == 1)
            def _():
                p_own[lax.rem(j, hn + 2), :, :, cols] = res[:, 1]
                p_send[slot, :, :, cols] = res[:, 0]
        sib(j).start()

    def reduce_step(s, j):
        slot = lax.rem(j, 2)
        if s == 0:
            sib(j).wait_recv()
        for d in range(2):
            free(functools.partial(rs, s, d), j)
            off = sign[d] * (hn - s)
            if s == 0:
                half_send[slot, d] = mine(j, off, rows_of[d]).astype(BF)
            else:
                rs(s - 1, d, j).wait_recv()
                if s == 1:
                    full_send[slot, 0, d, rows_of[1 - d]] = mine(j, off, rows_of[1 - d]).astype(BF)
                    full_send[slot, 0, d, rows_of[d]] = (
                        mine(j, off, rows_of[d]) + half_in[j, d].astype(F32)).astype(BF)
                else:
                    full_send[slot, s - 1, d] = (mine(j, off) + full_in[j, s - 2, d].astype(F32)).astype(BF)
            rs(s, d, j).start()

    def activate(j):
        @pl.when(j == 0)
        def _():
            sq = ss[pl.ds(pl.multiple_of(r * g, g), g), :]
            for d in range(1, nr):
                ss_copy(d).wait_recv()
                sq = sq + ssr[d - 1]
            mean = jnp.sum(sq, axis=1, keepdims=True) / total
            scale[...] = jnp.broadcast_to(lax.rsqrt(mean + 1e-5), scale.shape)
        for d in range(2):
            rs(hn - 1, d, j).wait_recv()
        val = mine(j, 0) + full_in[j, hn - 2, 0].astype(F32) + full_in[j, hn - 2, 1].astype(F32)
        val = val * scale[:, 0:1]
        gate, up = val[:, :w], val[:, w:]
        h_all[j, me, core] = (gate / (1.0 + jnp.exp(-gate)) * up).astype(BF)
        for d in range(2):
            free(functools.partial(ag, 0, d), j)
            ag(0, d, j).start()
        free(functools.partial(hs, 0), j)
        hs(0, j).start()

    def gather_step(s, j):
        for d in range(2):
            ag(s - 1, d, j, True).wait_recv()
            free(functools.partial(ag, s, d), j)
            ag(s, d, j).start()
            free(functools.partial(hs, -sign[d] * s), j)
            hs(-sign[d] * s, j).start()

    def gather_last(j):
        for d in range(2):
            ag(hn - 1, d, j, True).wait_recv()
        free(functools.partial(hs, hn), j)
        hs(hn, j).start()

    def down(j):
        slot = lax.rem(j, 2)

        @pl.when(j + 1 < chunks)
        def _():
            down_load(j + 1).start()
        down_load(j).wait()
        for off in range(n):
            hs(off, j, True).wait_recv()
        tile = 256

        @pl.loop(0, feat // tile)
        def _(t):
            cols = pl.ds(pl.multiple_of(t * tile, tile), tile)
            lhs = h_all[j].reshape(nr * g, w)
            res = jnp.dot(lhs, wdn[slot, :, cols], preferred_element_type=F32)
            acc[:, cols] += res

    acc[...] = jnp.zeros_like(acc)
    stages = [functools.partial(reduce_step, s) for s in range(hn)] + [activate]
    stages += [functools.partial(gather_step, s) for s in range(1, hn)] + [gather_last]
    order = [(1 + i, f) for i, f in enumerate(stages)]
    order += [(0, first), (1 + len(stages), down)]
    last = 1 + len(stages)

    @pl.loop(0, chunks + last)
    def _(t):
        for lag, stage in order:
            @pl.when((t >= lag) & (t - lag < chunks))
            def _():
                stage(t - lag)

    for j in (chunks - 2, chunks - 1):
        j = jnp.int32(j)
        sib(j).wait_send()
        for d in range(2):
            for s in range(hn):
                rs(s, d, j).wait_send()
                ag(s, d, j).wait_send()
        for off in range(n):
            hs(off, j).wait_send()

    def block(d):
        return pl.ds(pl.multiple_of(d * tr, tr), tr)

    def c_copy(s, d):
        src, dst = (cs_r, cr_r) if d == 0 else (cs_l, cr_l)
        return remote(src.at[s], dst.at[s], c_sems.at[0, d, s], c_sems.at[1, d, s], {"col": z + sign[d]})

    def c_wait(s, d):
        dst = cr_r if d == 0 else cr_l
        remote(dst.at[s], dst.at[s], c_sems.at[0, d, s], c_sems.at[1, d, s], {"col": z - sign[d]}).wait_recv()

    for s in range(nz - 1):
        for d in range(2):
            dest = nz - 1 - s if d == 0 else s
            src, got = (cs_r, cr_r) if d == 0 else (cs_l, cr_l)
            sends = z < dest if d == 0 else z > dest
            edge = z == (0 if d == 0 else nz - 1)

            @pl.when(sends & edge)
            def _():
                src[s] = acc[dest * tr:(dest + 1) * tr, :].astype(BF)
                c_copy(s, d).start()

            @pl.when(sends & jnp.logical_not(edge))
            def _():
                c_wait(s, d)
                src[s] = (acc[dest * tr:(dest + 1) * tr, :] + got[s].astype(F32)).astype(BF)
                c_copy(s, d).start()

    @pl.when(z > 0)
    def _():
        c_wait(nz - 1 - z, 0)
        acc[block(z), :] += cr_r[nz - 1 - z].astype(F32)

    @pl.when(z < nz - 1)
    def _():
        c_wait(z, 1)
        acc[block(z), :] += cr_l[z].astype(F32)

    out = (x_ref[...].astype(F32) + acc[block(z), :]).astype(BF)
    out_ref[...] = out
    diff = out.astype(F32) - teacher_ref[map_ref[0]].astype(F32)
    sq = jnp.sum((diff * diff).reshape(tr // 8, 8, feat), axis=0)
    part = sq[:, 0:128]
    for c in range(1, feat // 128):
        part = part + sq[:, c * 128:(c + 1) * 128]

    def l_copy(axis, d):
        size, at = (nr, r) if axis == "row" else (nz, z)
        src, dst = (lsum.at[0], l_row) if axis == "row" else (lsum.at[1], l_col)
        base = 0 if axis == "row" else nr - 1
        return remote(src, dst.at[d - 1], l_sems.at[0, base + d - 1], l_sems.at[1, base + d - 1],
                      {axis: lax.rem(at + d, size)})

    lsum[0] = part
    for d in range(1, nr):
        l_copy("row", d).start()
    for d in range(1, nr):
        l_copy("row", d).wait_recv()
        part = part + l_row[d - 1]
    lsum[1] = part
    for d in range(1, nz):
        l_copy("col", d).start()
    for d in range(1, nz):
        l_copy("col", d).wait_recv()
        part = part + l_col[d - 1]
    loss_ref[...] = part

    for d in range(1, nr):
        l_copy("row", d).wait_send()
        ss_copy(d).wait_send()
    for d in range(1, nz):
        l_copy("col", d).wait_send()
    for s in range(nz - 1):
        for d in range(2):
            @pl.when(x_sends(s, d))
            def _():
                x_copy(s, d).wait_send()
            dest = nz - 1 - s if d == 0 else s

            @pl.when(z < dest if d == 0 else z > dest)
            def _():
                c_copy(s, d).wait_send()


def body(nr, nz, student_in, norm_gain, w_gate, w_up, w_down, teacher, layer_map):
    tr, feat = student_in.shape
    ff = w_gate.shape[1]
    n, hn = nr // 2, nr // 4
    g = tr * nz // nr
    w = next(v for v in (512, 256, 128) if ff % v == 0)
    c = ff // w
    vm, dma = pltpu.VMEM, pltpu.SemaphoreType.DMA
    spec = pl.BlockSpec(memory_space=pltpu.VMEM)
    hbm = pl.BlockSpec(memory_space=pl.ANY)
    out, loss = pl.pallas_call(
        functools.partial(kernel, nr, nz, w, feat * nr),
        out_shape=(jax.ShapeDtypeStruct((tr, feat), BF), jax.ShapeDtypeStruct((8, 128), F32)),
        in_specs=[spec, spec, hbm, hbm, hbm, spec, pl.BlockSpec(memory_space=pltpu.SMEM)],
        out_specs=(spec, spec),
        scratch_shapes=[
            vm((nz, tr, feat), BF),
            vm((nz * tr, feat), BF),
            vm((nz * tr, 128), F32),
            vm((nr - 1, g, 128), F32),
            vm((g, 128), F32),
            vm((2, feat, 2 * w), BF),
            vm((2, w, feat), BF),
            vm((hn + 2, n, g, 2 * w), BF),
            vm((2, n, g, 2 * w), BF),
            vm((c, n, g, 2 * w), BF),
            vm((2, 2, g // 2, 2 * w), BF),
            vm((c, 2, g // 2, 2 * w), BF),
            vm((2, hn - 1, 2, g, 2 * w), BF),
            vm((c, hn - 1, 2, g, 2 * w), BF),
            vm((c, n, 2, g, w), BF),
            vm((nz * tr, feat), F32),
            vm((nz - 1, tr, feat), BF),
            vm((nz - 1, tr, feat), BF),
            vm((nz - 1, tr, feat), BF),
            vm((nz - 1, tr, feat), BF),
            vm((2, 8, 128), F32),
            vm((nr - 1, 8, 128), F32),
            vm((nz - 1, 8, 128), F32),
            dma((2, 2, nz - 1)),
            dma((2, 2)),
            dma((2,)),
            dma((2, nr - 1)),
            dma((2 + c,)),
            dma((hn, 2, 2)),
            dma((hn, 2, c)),
            dma((hn, 2, 2)),
            dma((hn, 2, c)),
            dma((n, 2)),
            dma((n, c)),
            dma((2, 2, nz - 1)),
            dma((2, nr + nz - 2)),
        ],
        compiler_params=pltpu.CompilerParams(
            collective_id=0, has_side_effects=True, vmem_limit_bytes=67043328),
    )(student_in, norm_gain.reshape(1, feat), w_gate, w_up, w_down, teacher, layer_map)
    return out, jnp.sum(loss) / (tr * nz * feat * nr)


def solution(mesh):
    placed = (
        P("col", "row"),
        P("row"),
        P("row", "col"),
        P("row", "col"),
        P("col", "row"),
        P(None, "col", "row"),
        P(),
    )
    return jax.shard_map(
        functools.partial(body, mesh.shape["row"], mesh.shape["col"]),
        mesh=mesh, in_specs=placed, out_specs=(P("col", "row"), P()), check_vma=False
    )
```

time: 429 us -> 236 us (0.55)
  waiting for transfers between devices: 277 us -> 0 us
  Pallas kernels: 0 us -> 229 us
  blocking collectives: 54.4 us -> 0 us
  matrix products: 54 us -> 0 us
  other arithmetic: 26.8 us -> 1.28 us
  between operations: 15.7 us -> 2.42 us
    pallas_call x0 -> x1, Pallas kernels: none -> 229 us  [body(): pl.pallas_call(functools.partial(kernel, nr, nz, w, feat * nr), out_shape...]
    reduce_scatter x2 -> x0, waiting for transfers between devices: 176 us -> none  [the longest x1 140 us: body(): lax.psum_scatter(jnp.concatenate([first, second], axis=1).astype(jnp.bflo...]
    all_gather x2 -> x0, waiting for transfers between devices: 102 us -> none  [the longest x1 65.2 us: body(): hidden_all = lax.all_gather(swiglu(mine, width), 'row', axis=0, tiled=True)]
    psum x2 -> x0, blocking collectives: 54.4 us -> none  [the longest x1 39.2 us: body(): total = lax.psum(jnp.sum(diff * diff), ('row', 'col'))]
    dot_general x3 -> x0, matrix products: 54 us -> none  [the longest x1 19 us: body(): first = jnp.dot(piece, w_gate, preferred_element_type=jnp.float32)]
    concatenate x1 -> x0, other arithmetic: 16.5 us -> none  [body(): jnp.concatenate([first, second], axis=1).astype(jnp.bfloat16)]
    convert_element_type x4 -> x0, other arithmetic: 6.64 us -> none  [the longest x1 2.26 us: body(): mine = lax.psum_scatter(jnp.concatenate([first, second], axis=1).astype(j...]
  transfers between devices with their start and end apart: 4 -> 0, of which waited for: 4 -> 0; matrix products, arithmetic and copies ran while one was open for 0% -> 0% of each run, Pallas kernels for 0% -> 0%
where the time goes in v1:
time: 236 us
  Pallas kernels  229 us (97%)
  local copies, waits for them, and re-layouts  3.05 us (1%)
  between operations  2.42 us (1%)
    pallas_call x1, Pallas kernels, body(): pl.pallas_call(functools.partial(kernel, nr, nz, w, feat * nr), out_shape...  229 us

profile of v1, /device:TPU:0, one launch (start us, length us, event | category | flops | bytes accessed | tf_op | source)
XLA Modules:
  0.0 235.9 jit_solution(8845285960963341214)
XLA Ops:
  0.6 1.3 reshape.7.gain_ref
  1.9 229.2 %shard_map.86 = (bf16[192,1024]{1,0:T(8,128)(2,1)}, f32[8,128]{1,0:T(8,128)}) custom-call(bf16[192,1024]{1,0:T(8,128)(2,1)} %x_ref.1, bf16[1,1024]{1,0:T(2,128)(2,1)} %reshape.7.gain_ref, bf16[1024,7168]{1,0:T(8,128)(2,1)} %wg_ref.1, bf16[1024,7168]{1,0:T(8,128)(2,1)} %wu_ref.1, bf16[7168,1024]{1,0:T(8,128)(2,1)} %wd_ref.1, ...), custom_call_target="tpu_custom_call" | custom-call | tf_op jit(solution)/shard_map/pallas_call | solution.py:381
  231.1 1.3 reduce_sum.9
  233.0 1.8 copy.10

commit v2 on v1

v2 whole, which is shorter than its diff:
```python
import functools

import jax
import jax.numpy as jnp
from jax import lax
from jax.experimental import pallas as pl
from jax.experimental.pallas import tpu as pltpu
from jax.sharding import PartitionSpec as P

BF = jnp.bfloat16
F32 = jnp.float32


def kernel(nr, nz, w, total, x_ref, gain_ref, wg_ref, wu_ref, wd_ref, teacher_ref, map_ref,
           out_ref, loss_ref,
           x_all, xg, ss, ssr, scale, wgu, wdn, p_own, p_send, s_in, half_send, half_in,
           full_send, full_in, h_all, acc, cs_r, cs_l, cr_r, cr_l, lsum, l_row, l_col,
           x_sems, w_sem, wd_sem, ss_sems, sib_sems, rs_send, rs_recv, ag_send, ag_recv,
           hs_send, hs_recv, c_sems, l_sems):
    chunks = s_in.shape[0]
    n = nr // 2
    hn = n // 2
    tr, feat = x_ref.shape
    th = tr // 2
    cn = chunks // 2
    g = th * nz // nr
    step = max(1, cn // (nz - 1))
    r = lax.axis_index("row")
    z = lax.axis_index("col")
    core = lax.rem(r, 2)
    chip = lax.div(r, 2)
    a, b = lax.div(chip, 2), lax.rem(chip, 2)
    pos = a + b * (n - 1 - 2 * a)

    def chip_at(off):
        q = lax.rem(pos + (off % n), n)
        far = lax.div(q, hn)
        return far * (2 * (n - 1 - q) + 1) + (1 - far) * 2 * q

    me = chip_at(0)
    sibling = {"row": chip * 2 + 1 - core}
    ring = ({"row": chip_at(1) * 2 + core}, {"row": chip_at(-1) * 2 + core})
    sign = (1, -1)
    pair_of = (slice(0, w), slice(w, 2 * w))
    unit_of = (pl.ds(0, w // 2), pl.ds(w // 2, w // 2))

    def remote(src, dst, send, recv, dev):
        return pltpu.make_async_remote_copy(
            src_ref=src, dst_ref=dst, send_sem=send, recv_sem=recv,
            device_id=dev, device_id_type=pl.DeviceIdType.MESH)

    barrier = pltpu.get_barrier_semaphore()
    for d in range(1, nr):
        pl.semaphore_signal(barrier, inc=1, device_id={"row": lax.rem(r + d, nr)},
                            device_id_type=pl.DeviceIdType.MESH)
    for d in range(1, nz):
        pl.semaphore_signal(barrier, inc=1, device_id={"col": lax.rem(z + d, nz)},
                            device_id_type=pl.DeviceIdType.MESH)
    pl.semaphore_wait(barrier, nr - 1 + nz - 1)

    def up_load(j):
        slot = lax.rem(j, 2)
        cols = pl.ds(pl.multiple_of(lax.rem(j, cn) * w, w), w)
        return (pltpu.make_async_copy(wg_ref.at[:, cols], wgu.at[slot, :, pl.ds(0, w)], w_sem.at[slot, 0]),
                pltpu.make_async_copy(wu_ref.at[:, cols], wgu.at[slot, :, pl.ds(w, w)], w_sem.at[slot, 1]))

    def down_load(j):
        slot = lax.rem(j, 2)
        return pltpu.make_async_copy(wd_ref.at[pl.ds(pl.multiple_of(lax.rem(j, cn) * w, w), w)], wdn.at[slot], wd_sem.at[slot])

    for c in up_load(jnp.int32(0)):
        c.start()
    down_load(jnp.int32(0)).start()

    gain = gain_ref[...].astype(F32)

    def own(hf):
        return x_ref.at[pl.ds(hf * th, th)]

    def absorb(src, hf, blk):
        xf = src[...].astype(F32)
        rows = pl.ds(pl.multiple_of(blk * th, th), th)
        xg[hf, rows, :] = (xf * gain).astype(BF)
        sq = xf * xf
        part = sq[:, 0:128]
        for c in range(1, feat // 128):
            part = part + sq[:, c * 128:(c + 1) * 128]
        ss[hf, rows, :] = part

    def x_copy(hf, s, d):
        blk = z - s * sign[d]
        src = own(hf) if s == 0 else x_all.at[hf, blk]
        return remote(src, x_all.at[hf, blk], x_sems.at[0, hf, d, s], x_sems.at[1, hf, d, s],
                      {"col": z + sign[d]})

    def x_sends(s, d):
        return (z < nz - 1) & (z - s >= 0) if d == 0 else (z > 0) & (z + s <= nz - 1)

    def x_gets(s, d):
        return z - 1 - s >= 0 if d == 0 else z + 1 + s <= nz - 1

    def x_wait(hf, s, d):
        ref = x_all.at[hf, z - (s + 1) * sign[d]]
        remote(ref, ref, x_sems.at[0, hf, d, s], x_sems.at[1, hf, d, s], {"col": z - sign[d]}).wait_recv()

    def x_step(hf, s):
        for d in range(2):
            if s > 0:
                @pl.when(x_gets(s - 1, d))
                def _():
                    x_wait(hf, s - 1, d)
            if s < nz - 1:
                @pl.when(x_sends(s, d))
                def _():
                    x_copy(hf, s, d).start()

    def x_absorb(hf, s):
        if s == 0:
            absorb(own(hf), hf, z)
        else:
            for d in range(2):
                @pl.when(x_gets(s - 1, d))
                def _():
                    absorb(x_all.at[hf, z - s * sign[d]], hf, z - s * sign[d])

    def ss_copy(hf, d):
        peer = lax.rem(r + d, nr)
        return remote(ss.at[hf, pl.ds(pl.multiple_of(peer * g, g), g)], ssr.at[hf, d - 1],
                      ss_sems.at[0, hf, d - 1], ss_sems.at[1, hf, d - 1], {"row": peer})

    def ss_start(hf):
        for d in range(1, nr):
            ss_copy(hf, d).start()

    for s in range(nz):
        x_step(0, s)
        if s == nz - 1:
            x_step(1, 0)
        x_absorb(0, s)
        if s == 0:
            x_absorb(1, 0)
            acc[...] = jnp.zeros_like(acc)
    ss_start(0)

    def sib(j):
        slot = lax.rem(j, 2)
        return remote(p_send.at[slot], s_in.at[j], sib_sems.at[slot], sib_sems.at[2 + j], sibling)

    def rs(s, d, j):
        slot = lax.rem(j, 2)
        if s == 0:
            src, dst = half_send.at[slot, d], half_in.at[j, d]
        else:
            src, dst = full_send.at[slot, s - 1, d], full_in.at[j, s - 1, d]
        return remote(src, dst, rs_send.at[s, d, slot], rs_recv.at[s, d, j], ring[d])

    def ag(s, d, j, got=False):
        blk = chip_at(-sign[d] * (s + 1 if got else s))
        ref = h_all.at[j, blk, core]
        if s == hn - 1:
            ref = h_all.at[j, blk, core, :, unit_of[d]]
        return remote(ref, ref, ag_send.at[s, d, lax.rem(j, 2)], ag_recv.at[s, d, j], ring[d])

    def hs(off, j, got=False):
        ref = h_all.at[j, chip_at(off), 1 - core if got else core]
        return remote(ref, ref, hs_send.at[off % n, lax.rem(j, 2)], hs_recv.at[off % n, j], sibling)

    def free(make, j):
        @pl.when(j >= 2)
        def _():
            make(j - 2).wait_send()

    def mine(j, off, cols=slice(None)):
        q = chip_at(off)
        return (p_own[lax.rem(j, hn + 2), q, :, cols].astype(F32) + s_in[j, q, :, cols].astype(F32))

    def first(j):
        slot = lax.rem(j, 2)

        @pl.when(j + 1 < chunks)
        def _():
            for c in up_load(j + 1):
                c.start()
        for c in up_load(j):
            c.wait()
        free(sib, j)
        tile = 256

        @pl.loop(0, 2 * w // tile)
        def _(t):
            cols = pl.ds(pl.multiple_of(t * tile, tile), tile)
            res = jnp.dot(xg[lax.div(j, cn)], wgu[slot, :, cols], preferred_element_type=F32).astype(BF)
            res = res.reshape(n, 2, g, tile)

            @pl.when(core == 0)
            def _():
                p_own[lax.rem(j, hn + 2), :, :, cols] = res[:, 0]
                p_send[slot, :, :, cols] = res[:, 1]

            @pl.when(core == 1)
            def _():
                p_own[lax.rem(j, hn + 2), :, :, cols] = res[:, 1]
                p_send[slot, :, :, cols] = res[:, 0]
        sib(j).start()

    def reduce_step(s, j):
        slot = lax.rem(j, 2)
        if s == 0:
            sib(j).wait_recv()
        for d in range(2):
            free(functools.partial(rs, s, d), j)
            off = sign[d] * (hn - s)
            if s == 0:
                half_send[slot, d] = mine(j, off, pair_of[d]).astype(BF)
            else:
                rs(s - 1, d, j).wait_recv()
                if s == 1:
                    full_send[slot, 0, d, :, pair_of[1 - d]] = mine(j, off, pair_of[1 - d]).astype(BF)
                    full_send[slot, 0, d, :, pair_of[d]] = (
                        mine(j, off, pair_of[d]) + half_in[j, d].astype(F32)).astype(BF)
                else:
                    full_send[slot, s - 1, d] = (mine(j, off) + full_in[j, s - 2, d].astype(F32)).astype(BF)
            rs(s, d, j).start()

    def activate(j):
        for hf in range(2):
            @pl.when(j == hf * cn)
            def _():
                sq = ss[hf, pl.ds(pl.multiple_of(r * g, g), g), :]
                for d in range(1, nr):
                    ss_copy(hf, d).wait_recv()
                    sq = sq + ssr[hf, d - 1]
                mean = jnp.sum(sq, axis=1, keepdims=True) / total
                scale[hf] = jnp.broadcast_to(lax.rsqrt(mean + 1e-5), (g, 128))
        for d in range(2):
            rs(hn - 1, d, j).wait_recv()
        val = mine(j, 0) + full_in[j, hn - 2, 0].astype(F32) + full_in[j, hn - 2, 1].astype(F32)
        val = val * scale[lax.div(j, cn)][:, 0:1]
        gate, up = val[:, :w], val[:, w:]
        h_all[j, me, core] = (gate / (1.0 + jnp.exp(-gate)) * up).astype(BF)
        for d in range(2):
            free(functools.partial(ag, 0, d), j)
            ag(0, d, j).start()
        free(functools.partial(hs, 0), j)
        hs(0, j).start()

    def gather_step(s, j):
        for d in range(2):
            ag(s - 1, d, j, True).wait_recv()
            free(functools.partial(ag, s, d), j)
            ag(s, d, j).start()
            free(functools.partial(hs, -sign[d] * s), j)
            hs(-sign[d] * s, j).start()

    def gather_last(j):
        for d in range(2):
            ag(hn - 1, d, j, True).wait_recv()
        free(functools.partial(hs, hn), j)
        hs(hn, j).start()

    def down(j):
        slot = lax.rem(j, 2)

        @pl.when(j + 1 < chunks)
        def _():
            down_load(j + 1).start()
        down_load(j).wait()
        for off in range(n):
            hs(off, j, True).wait_recv()
        tile = 256

        @pl.loop(0, feat // tile)
        def _(t):
            cols = pl.ds(pl.multiple_of(t * tile, tile), tile)
            lhs = h_all[j].reshape(nr * g, w)
            res = jnp.dot(lhs, wdn[slot, :, cols], preferred_element_type=F32)
            acc[lax.div(j, cn), :, cols] += res

    stages = [functools.partial(reduce_step, s) for s in range(hn)] + [activate]
    stages += [functools.partial(gather_step, s) for s in range(1, hn)] + [gather_last]
    order = [(1 + i, f) for i, f in enumerate(stages)]
    order += [(0, first), (1 + len(stages), down)]
    last = 1 + len(stages)

    def c_refs(hf, d):
        return (cs_r.at[hf], cr_r.at[hf]) if d == 0 else (cs_l.at[hf], cr_l.at[hf])

    def c_copy(hf, s, d):
        src, dst = c_refs(hf, d)
        return remote(src.at[s], dst.at[s], c_sems.at[0, hf, d, s], c_sems.at[1, hf, d, s], {"col": z + sign[d]})

    def c_wait(hf, s, d):
        dst = c_refs(hf, d)[1]
        remote(dst.at[s], dst.at[s], c_sems.at[0, hf, d, s], c_sems.at[1, hf, d, s],
               {"col": z - sign[d]}).wait_recv()

    def c_sends(s, d):
        return z < nz - 1 - s if d == 0 else z > s

    def c_step(hf, s, d):
        dest = nz - 1 - s if d == 0 else s
        src, got = c_refs(hf, d)
        edge = z == (0 if d == 0 else nz - 1)

        @pl.when(c_sends(s, d) & edge)
        def _():
            src[s] = acc[hf, dest * th:(dest + 1) * th, :].astype(BF)
            c_copy(hf, s, d).start()

        @pl.when(c_sends(s, d) & jnp.logical_not(edge))
        def _():
            c_wait(hf, s, d)
            src[s] = (acc[hf, dest * th:(dest + 1) * th, :] + got[s].astype(F32)).astype(BF)
            c_copy(hf, s, d).start()

    def c_last(hf):
        block = pl.ds(pl.multiple_of(z * th, th), th)

        @pl.when(z > 0)
        def _():
            c_wait(hf, nz - 1 - z, 0)
            acc[hf, block, :] += cr_r[hf, nz - 1 - z].astype(F32)

        @pl.when(z < nz - 1)
        def _():
            c_wait(hf, z, 1)
            acc[hf, block, :] += cr_l[hf, z].astype(F32)

        rows = slice(hf * th, (hf + 1) * th)
        out = (x_ref[rows, :].astype(F32) + acc[hf, block, :]).astype(BF)
        out_ref[rows, :] = out
        diff = out.astype(F32) - teacher_ref[map_ref[0], rows, :].astype(F32)
        sq = jnp.sum((diff * diff).reshape(th // 8, 8, feat), axis=0)
        part = sq[:, 0:128]
        for c in range(1, feat // 128):
            part = part + sq[:, c * 128:(c + 1) * 128]
        return part

    pace = cn // (2 * nz - 3)

    @pl.loop(0, chunks + last)
    def _(t):
        for s in range(1, nz):
            @pl.when(t == s * step)
            def _():
                x_step(1, s)
                x_absorb(1, s)
                if s == nz - 1:
                    ss_start(1)
        for lag, stage in order:
            @pl.when((t >= lag) & (t - lag < chunks))
            def _():
                stage(t - lag)
        for s in range(nz - 1):
            for d in range(2):
                hop = z if d == 0 else nz - 1 - z
                at = pace * (s + hop) if pace > 0 else s

                @pl.when(t == cn + last + at)
                def _():
                    c_step(0, s, d)

    for s in range(nz - 1):
        for d in range(2):
            c_step(1, s, d)
        if s == 0:
            part = c_last(0)
    part = part + c_last(1)

    def l_copy(axis, d):
        size, at = (nr, r) if axis == "row" else (nz, z)
        src, dst = (lsum.at[0], l_row) if axis == "row" else (lsum.at[1], l_col)
        base = 0 if axis == "row" else nr - 1
        return remote(src, dst.at[d - 1], l_sems.at[0, base + d - 1], l_sems.at[1, base + d - 1],
                      {axis: lax.rem(at + d, size)})

    lsum[0] = part
    for d in range(1, nr):
        l_copy("row", d).start()
    for d in range(1, nr):
        l_copy("row", d).wait_recv()
        part = part + l_row[d - 1]
    lsum[1] = part
    for d in range(1, nz):
        l_copy("col", d).start()
    for d in range(1, nz):
        l_copy("col", d).wait_recv()
        part = part + l_col[d - 1]
    loss_ref[...] = part

    for d in range(1, nr):
        l_copy("row", d).wait_send()
        for hf in range(2):
            ss_copy(hf, d).wait_send()
    for d in range(1, nz):
        l_copy("col", d).wait_send()
    for s in range(nz - 1):
        for d in range(2):
            @pl.when(x_sends(s, d))
            def _():
                for hf in range(2):
                    x_copy(hf, s, d).wait_send()

            @pl.when(c_sends(s, d))
            def _():
                for hf in range(2):
                    c_copy(hf, s, d).wait_send()
    for j in (chunks - 2, chunks - 1):
        j = jnp.int32(j)
        sib(j).wait_send()
        for d in range(2):
            for s in range(hn):
                rs(s, d, j).wait_send()
                ag(s, d, j).wait_send()
        for off in range(n):
            hs(off, j).wait_send()


def body(nr, nz, student_in, norm_gain, w_gate, w_up, w_down, teacher, layer_map):
    tr, feat = student_in.shape
    ff = w_gate.shape[1]
    n, hn = nr // 2, nr // 4
    th = tr // 2
    g = th * nz // nr
    w = next(v for v in (512, 256, 128) if ff % v == 0)
    c = 2 * (ff // w)
    vm, dma = pltpu.VMEM, pltpu.SemaphoreType.DMA
    spec = pl.BlockSpec(memory_space=pltpu.VMEM)
    hbm = pl.BlockSpec(memory_space=pl.ANY)
    out, loss = pl.pallas_call(
        functools.partial(kernel, nr, nz, w, feat * nr),
        out_shape=(jax.ShapeDtypeStruct((tr, feat), BF), jax.ShapeDtypeStruct((8, 128), F32)),
        in_specs=[spec, spec, hbm, hbm, hbm, spec, pl.BlockSpec(memory_space=pltpu.SMEM)],
        out_specs=(spec, spec),
        scratch_shapes=[
            vm((2, nz, th, feat), BF),
            vm((2, nz * th, feat), BF),
            vm((2, nz * th, 128), F32),
            vm((2, nr - 1, g, 128), F32),
            vm((2, g, 128), F32),
            vm((2, feat, 2 * w), BF),
            vm((2, w, feat), BF),
            vm((hn + 2, n, g, 2 * w), BF),
            vm((2, n, g, 2 * w), BF),
            vm((c, n, g, 2 * w), BF),
            vm((2, 2, g, w), BF),
            vm((c, 2, g, w), BF),
            vm((2, hn - 1, 2, g, 2 * w), BF),
            vm((c, hn - 1, 2, g, 2 * w), BF),
            vm((c, n, 2, g, w), BF),
            vm((2, nz * th, feat), F32),
            vm((2, nz - 1, th, feat), BF),
            vm((2, nz - 1, th, feat), BF),
            vm((2, nz - 1, th, feat), BF),
            vm((2, nz - 1, th, feat), BF),
            vm((2, 8, 128), F32),
            vm((nr - 1, 8, 128), F32),
            vm((nz - 1, 8, 128), F32),
            dma((2, 2, 2, nz - 1)),
            dma((2, 2)),
            dma((2,)),
            dma((2, 2, nr - 1)),
            dma((2 + c,)),
            dma((hn, 2, 2)),
            dma((hn, 2, c)),
            dma((hn, 2, 2)),
            dma((hn, 2, c)),
            dma((n, 2)),
            dma((n, c)),
            dma((2, 2, 2, nz - 1)),
            dma((2, nr + nz - 2)),
        ],
        compiler_params=pltpu.CompilerParams(
            collective_id=0, has_side_effects=True, vmem_limit_bytes=67043328),
    )(student_in, norm_gain.reshape(1, feat), w_gate, w_up, w_down, teacher, layer_map)
    return out, jnp.sum(loss) / (tr * nz * feat * nr)


def solution(mesh):
    placed = (
        P("col", "row"),
        P("row"),
        P("row", "col"),
        P("row", "col"),
        P("col", "row"),
        P(None, "col", "row"),
        P(),
    )
    return jax.shard_map(
        functools.partial(body, mesh.shape["row"], mesh.shape["col"]),
        mesh=mesh, in_specs=placed, out_specs=(P("col", "row"), P()), check_vma=False
    )
```

time: 236 us -> 223 us (0.945)
  Pallas kernels: 229 us -> 216 us
    pallas_call x1, Pallas kernels: 229 us -> 216 us  [body(): pl.pallas_call(functools.partial(kernel, nr, nz, w, feat * nr), out_shape...]
where the time goes in v2:
time: 223 us
  Pallas kernels  216 us (97%)
  local copies, waits for them, and re-layouts  3.05 us (1%)
  between operations  2.42 us (1%)
    pallas_call x1, Pallas kernels, body(): pl.pallas_call(functools.partial(kernel, nr, nz, w, feat * nr), out_shape...  216 us

profile of v2, /device:TPU:0, one launch (start us, length us, event | category | flops | bytes accessed | tf_op | source)
XLA Modules:
  0.0 222.6 jit_solution(8551793156326812273)
XLA Ops:
  0.6 1.3 reshape.7.gain_ref
  1.9 215.9 %shard_map.86 = (bf16[192,1024]{1,0:T(8,128)(2,1)}, f32[8,128]{1,0:T(8,128)}) custom-call(bf16[192,1024]{1,0:T(8,128)(2,1)} %x_ref.1, bf16[1,1024]{1,0:T(2,128)(2,1)} %reshape.7.gain_ref, bf16[1024,7168]{1,0:T(8,128)(2,1)} %wg_ref.1, bf16[1024,7168]{1,0:T(8,128)(2,1)} %wu_ref.1, bf16[7168,1024]{1,0:T(8,128)(2,1)} %wd_ref.1, ...), custom_call_target="tpu_custom_call" | custom-call | tf_op jit(solution)/shard_map/pallas_call | solution.py:430
  217.8 1.3 reduce_sum.9
  219.7 1.8 copy.10
